TPU v7x, 256 devices: a whole 4x4x8 slice. The times are simulated.
256 devices in a mesh: rows: 8 (over x, core), protos: 32 (over y, z).
Axes of the slice: x: 4, y: 4, z: 8, core: 2. Of those that a mesh axis runs over, the one named last changes fastest.
Arguments:
- teacher_features: bfloat16 [4096, 384], P(('rows', 'protos')), may hold values from -80 to 80, as said below
- student_features: bfloat16 [4096, 384], P(('rows', 'protos')), may hold values from -80 to 80, as said below
- prototypes: bfloat16 [131072, 384], P('protos'), may hold values from -80 to 80, as said below
Outputs:
- feature_grad: float32 [4096, 384], P(('rows', 'protos'))
- proto_grad: float32 [8, 16384, 384], P('rows', 'protos')
Inputs may be any that keep to these rules, and one draw needn't show every extreme that they name: `teacher_features`: every row has nonzero entries. `student_features`: every row has nonzero entries. `prototypes`: every row has nonzero entries.
All inputs are finite; a program needn't handle non-finite values.
Results may differ from a plain program's by a relative error of at most 0.012.
The roundings to bfloat16 on the way count: a program that leaves them out, or rounds other values in their place, can miss the bound.
Values may be sent and summed in bfloat16 or wider, within the bound.
A program may use at most 64 MiB of HBM per device.

v0:
```python
import math
import jax
import jax.numpy as jnp
from jax import lax
from jax.sharding import PartitionSpec as P

D = 384
K = 131072
PASSES = 3
eps = 1e-06


def unitize(values):
    values = values.astype(jnp.float32)
    return (values * lax.rsqrt(jnp.sum(values * values, axis=1, keepdims=True) + eps)).astype(
        jnp.bfloat16
    )


def against(left, right):
    return lax.dot_general(
        left, right, (((1,), (1,)), ((), ())), preferred_element_type=jnp.float32
    )


def on_device(teacher_features, student_features, prototypes):
    scale = 1.5 * math.sqrt(D)
    unit_w = unitize(prototypes)
    local_t = unitize(teacher_features)
    local_s = unitize(student_features)
    unit_t, unit_s = (
        lax.all_gather(local_t, "protos", axis=0, tiled=True),
        lax.all_gather(local_s, "protos", axis=0, tiled=True),
    )
    kernel = jnp.exp(scale * against(unit_t, unit_w))
    powers = jnp.exp(scale * against(unit_s, unit_w))
    student_part = jnp.sum(powers, axis=1)
    student_whole = lax.psum(student_part, "protos")
    row_scale = jnp.ones((kernel.shape[0],), jnp.float32)
    col_scale = jnp.ones((kernel.shape[1],), jnp.float32)
    for step in range(PASSES):
        col_part = jnp.dot(row_scale, kernel, precision=lax.Precision.HIGHEST)
        col_scale = 1.0 / lax.psum(col_part, "rows")
        row_part = jnp.dot(kernel, col_scale, precision=lax.Precision.HIGHEST)
        if step == 0:
            row_whole = lax.psum(row_part, "protos")
        else:
            row_whole = lax.psum(row_part, "protos")
        row_scale = 1.0 / row_whole
    target = kernel * row_scale[:, None] * col_scale[None, :]
    probs = powers / student_whole[:, None]
    delta = (probs - target).astype(jnp.bfloat16)
    feature_term = scale * jnp.dot(delta, unit_w, preferred_element_type=jnp.float32)
    feature_grad = lax.psum_scatter(feature_term, "protos", scatter_dimension=0, tiled=True)
    row_groups = lax.axis_size("rows")
    total_rows = delta.shape[0] * row_groups
    factor = scale * K / total_rows
    block = delta.shape[1] // row_groups
    term = factor * lax.dot_general(
        delta, unit_s, (((0,), (0,)), ((), ())), preferred_element_type=jnp.float32
    )
    proto_grad = lax.psum_scatter(
        term.reshape(row_groups, block, term.shape[1]), "rows", scatter_dimension=0, tiled=True
    )
    return (feature_grad, proto_grad)


def solution(mesh):
    return jax.shard_map(
        on_device,
        mesh=mesh,
        in_specs=(P(("rows", "protos"), None), P(("rows", "protos"), None), P("protos", None)),
        out_specs=(P(("rows", "protos"), None), P("rows", "protos", None)),
        check_vma=False,
    )
```

profile of v0, /device:TPU:1, one launch (start us, length us, event | category | flops | bytes accessed | tf_op | source)
XLA Modules:
  0.0 735.6 jit_solution(5828482277272511359)
XLA Ops:
  7.2 0.0 reduce-scatter.3.cloned.1.call-start
  7.2 0.8 fusion.5
  8.0 0.8 fusion.3
  8.9 0.8 fusion.4
  9.7 0.8 fusion.6
  10.4 2.6 fusion.1
  13.0 0.0 copy-start.3
  13.1 41.6 %all_gather.6 = bf16[512,384]{1,0:T(8,128)(2,1)S(1)} all-gather(bf16[16,384]{1,0:T(8,128)(2,1)S(1)} %fusion.4), channel_id=1, replica_groups=mesh['rows'=8,'protos'=32] {'protos'}, dimensions={0}, use_global_device_ids=true | all-gather | bytes 405504 | tf_op jit(solution)/shard_map/all_gather | solution.py:33
  54.6 36.7 %all_gather.7 = bf16[512,384]{1,0:T(8,128)(2,1)S(1)} all-gather(bf16[16,384]{1,0:T(8,128)(2,1)S(1)} %fusion.6), channel_id=1, replica_groups=mesh['rows'=8,'protos'=32] {'protos'}, dimensions={0}, use_global_device_ids=true | all-gather | bytes 405504 | tf_op jit(solution)/shard_map/all_gather | solution.py:32
  91.3 4.3 multiply_exponential_fusion
  95.7 0.0 copy-start
  95.7 3.2 copy-done
  98.9 4.0 fusion.7
  102.9 0.0 copy-done.3
  102.9 44.7 %psum.50 = f32[4096]{0:T(1024)S(1)} all-reduce(f32[4096]{0:T(1024)S(1)} %bitcast.34), channel_id=1, replica_groups=mesh['rows'=8,'protos'=32] {'rows'}, use_global_device_ids=true, to_apply=%region_5.0 | all-reduce | flops 4096 | bytes 32768 | tf_op jit(solution)/shard_map/psum | solution.py:43
  147.7 9.4 %fusion.14 = f32[1,512]{1,0:T(1,128)S(1)} fusion(f32[512,4096]{1,0:T(8,128)} %copy-done, f32[4096,1]{0,1:T(1,128)S(1)} %bitcast.30), kind=kOutput, calls=%fused_computation.31 | convolution fusion | flops 25165824 | bytes 8407040 | tf_op jit(solution)/shard_map/dot_general | solution.py:44
  157.1 58.6 %psum.51 = f32[512]{0:T(512)S(1)} all-reduce(f32[512]{0:T(512)S(1)} %bitcast.36), channel_id=1, replica_groups=mesh['rows'=8,'protos'=32] {'protos'}, use_global_device_ids=true, to_apply=%region_6.0 | all-reduce | flops 512 | bytes 4096 | tf_op jit(solution)/shard_map/psum | solution.py:46
  215.7 6.3 fusion.15
  222.1 37.4 %psum.52 = f32[4096]{0:T(1024)S(1)} all-reduce(f32[4096]{0:T(1024)S(1)} %bitcast.31), channel_id=1, replica_groups=mesh['rows'=8,'protos'=32] {'rows'}, use_global_device_ids=true, to_apply=%region_7.0 | all-reduce | flops 4096 | bytes 32768 | tf_op jit(solution)/shard_map/psum | solution.py:43
  259.5 9.4 %fusion.16 = f32[1,512]{1,0:T(1,128)S(1)} fusion(f32[512,4096]{1,0:T(8,128)} %copy-done, f32[4096,1]{0,1:T(1,128)S(1)} %bitcast.32), kind=kOutput, calls=%fused_computation.33 | convolution fusion | flops 25165824 | bytes 8407040 | tf_op jit(solution)/shard_map/dot_general | solution.py:44
  268.9 55.8 %psum.53 = f32[512]{0:T(512)S(1)} all-reduce(f32[512]{0:T(512)S(1)} %bitcast.38), channel_id=1, replica_groups=mesh['rows'=8,'protos'=32] {'protos'}, use_global_device_ids=true, to_apply=%region_8.0 | all-reduce | flops 512 | bytes 4096 | tf_op jit(solution)/shard_map/psum | solution.py:48
  324.7 0.0 copy-start.1
  324.7 6.5 fusion.17
  331.2 37.6 %psum.54 = f32[4096]{0:T(1024)} all-reduce(f32[4096]{0:T(1024)S(1)} %bitcast.33), channel_id=1, replica_groups=mesh['rows'=8,'protos'=32] {'rows'}, use_global_device_ids=true, to_apply=%region_9.0 | all-reduce | flops 4096 | bytes 32768 | tf_op jit(solution)/shard_map/psum | solution.py:43
  368.8 0.7 broadcast_divide_fusion
  369.6 10.0 %fusion.18 = f32[1,512]{1,0:T(1,128)} fusion(f32[512,4096]{1,0:T(8,128)} %copy-done, f32[4096,1]{0,1:T(1,128)S(1)} %bitcast.29), kind=kOutput, calls=%fused_computation.35 | convolution fusion | flops 25165824 | bytes 8407040 | tf_op jit(solution)/shard_map/dot_general | solution.py:44
  379.6 0.0 copy-done.1
  379.6 6.2 fusion
  385.8 58.2 %all-reduce = (f32[512]{0:T(512)}, f32[512]{0:T(512)}) all-reduce(f32[512]{0:T(512)} %bitcast.35, f32[512]{0:T(512)} %get-tuple-element.4), channel_id=1, replica_groups=mesh['rows'=8,'protos'=32] {'protos'}, use_global_device_ids=true, to_apply=%region_10.0 | all-reduce | flops 1024 | bytes 8192 | tf_op jit(solution)/shard_map/psum | solution.py:48
  444.0 0.7 broadcast_divide_fusion.5
  444.6 0.0 copy-start.4
  444.6 7.3 subtract_convert_fusion
  452.0 0.0 copy-start.2
  452.0 2.0 copy-done.2
  454.0 0.0 copy-done.4
  454.0 3.3 convolution_multiply_fusion.1
  457.4 0.0 reduce-scatter.3.cloned.1.call-update
  457.4 0.0 reduce-scatter.5.cloned.1.call-start
  457.4 7.2 convolution_multiply_fusion
  464.7 0.0 reduce-scatter.5.cloned.1.call-update
  464.7 212.9 %reduce-scatter.3.cloned.1.call-done = f32[16,384]{1,0:T(8,128)} async-done(((f32[512,384]{1,0:T(8,128)}), f32[16,384]{1,0:T(8,128)}) %reduce-scatter.3.cloned.1.call-update) | async-done | bytes 24592 | tf_op jit(solution)/shard_map/reduce_scatter | solution.py:54
  677.6 51.2 %reduce-scatter.5.cloned.1.call-done = f32[1,512,384]{2,1,0:T(8,128)} async-done(((f32[8,512,384]{2,1,0:T(8,128)}), f32[1,512,384]{2,1,0:T(8,128)}) %reduce-scatter.5.cloned.1.call-update) | async-done | bytes 786448 | tf_op jit(solution)/shard_map/reduce_scatter | solution.py:62
  (7 shorter events, 0.0 us)
Async XLA Ops:
  7.2 670.4 %reduce-scatter.3.cloned.1.call-start = ((), (), s32[]{:S(2)}) async-start(), calls=%async_computation.2 | async-start | bytes 811008 | tf_op jit(solution)/shard_map/reduce_scatter | solution.py:54
  13.0 89.9 %copy-start.3 = (f32[4096]{0:T(1024)}, f32[4096]{0:T(1024)S(1)}, u32[]{:S(2)}) copy-start(f32[4096]{0:T(1024)S(1)} %add_rsqrt_fusion) | copy-start | bytes 49156
  95.7 3.2 copy-start
  324.7 54.9 %copy-start.1 = (bf16[4096,384]{1,0:T(8,128)(2,1)S(1)}, bf16[4096,384]{1,0:T(8,128)(2,1)}, u32[]{:S(2)}) copy-start(bf16[4096,384]{1,0:T(8,128)(2,1)} %param.5) | copy-start | bytes 9437188
  444.6 9.4 %copy-start.4 = (f32[4096]{0:T(1024)S(1)}, f32[4096]{0:T(1024)}, u32[]{:S(2)}) copy-start(f32[4096]{0:T(1024)} %copy-done.3) | copy-start | bytes 49156
  452.0 2.0 copy-start.2
  457.4 271.4 %reduce-scatter.5.cloned.1.call-start = ((), (), s32[]{:S(2)}) async-start(), calls=%async_computation.3 | async-start | bytes 7077888 | tf_op jit(solution)/shard_map/reduce_scatter | solution.py:62
Sparse Core Ops, SparseCore 0:
  457.5 220.0 reduce-scatter.2
  680.7 48.0 reduce-scatter.4
where the time goes:
time: 736 us
  blocking collectives  371 us (50%)
  waiting for transfers between devices  264 us (36%)
  matrix products  66.9 us (9%)
  other arithmetic  14.6 us (2%)
  between operations  14.1 us (2%)
    reduce_scatter x1, waiting for transfers between devices, on_device(): lax.psum_scatter(feature_term, 'protos', scatter_dimension=0, tiled=True)  213 us
    psum x3, blocking collectives, on_device(): row_whole = lax.psum(row_part, 'protos')  173 us
    psum x3, blocking collectives, on_device(): col_scale = 1.0 / lax.psum(col_part, 'rows')  120 us
    reduce_scatter x1, waiting for transfers between devices, on_device(): lax.psum_scatter(term.reshape(row_groups, block, term.shape[1]), 'rows',...  51.2 us
    all_gather x1, blocking collectives, on_device(): lax.all_gather(local_s, 'protos', axis=0, tiled=True)  41.6 us
    all_gather x1, blocking collectives, on_device(): lax.all_gather(local_t, 'protos', axis=0, tiled=True)  36.7 us
    dot_general x3, matrix products, on_device(): row_part = jnp.dot(kernel, col_scale, precision=lax.Precision.HIGHEST)  28.9 us
    dot_general x3, matrix products, on_device(): col_part = jnp.dot(row_scale, kernel, precision=lax.Precision.HIGHEST)  16.9 us
  transfers between devices with their start and end apart: 2, of which 2 were waited for; matrix products, arithmetic and copies ran while one was open for 1% of the time, Pallas kernels for 0%

commit v1 on v0

--- a/solution.py
+++ b/solution.py
@@ -1,13 +1,24 @@
+import functools
 import math
 import jax
 import jax.numpy as jnp
 from jax import lax
 from jax.sharding import PartitionSpec as P
+from jax.lax import all_to_all, axis_size
 
 D = 384
 K = 131072
 PASSES = 3
 eps = 1e-06
+
+
+def hold_stacks_all(t0, pos_dim):
+    known = axis_size("protos")
+    back = jnp.concatenate(known * [t0], axis=pos_dim)
+    return all_to_all(back, "protos", pos_dim, pos_dim, tiled=True)
+
+
+unite_signs = functools.partial(hold_stacks_all, pos_dim=0)
 
 
 def unitize(values):
@@ -28,10 +39,7 @@
     unit_w = unitize(prototypes)
     local_t = unitize(teacher_features)
     local_s = unitize(student_features)
-    unit_t, unit_s = (
-        lax.all_gather(local_t, "protos", axis=0, tiled=True),
-        lax.all_gather(local_s, "protos", axis=0, tiled=True),
-    )
+    unit_t, unit_s = (lax.all_gather(local_t, "protos", axis=0, tiled=True), unite_signs(local_s))
     kernel = jnp.exp(scale * against(unit_t, unit_w))
     powers = jnp.exp(scale * against(unit_s, unit_w))
     student_part = jnp.sum(powers, axis=1)

time: 736 us -> 743 us (level)
  blocking collectives: 371 us -> 319 us
  other arithmetic: 14.6 us -> 57.9 us
  starting transfers between devices: 0.08 us -> 12.1 us
    unnamed x0 -> x31, other arithmetic: none -> 42.7 us
    all_gather x1 -> x0, blocking collectives: 41.6 us -> none  [on_device(): lax.all_gather(local_s, 'protos', axis=0, tiled=True)]
    all_to_all x0 -> x1, starting transfers between devices: none -> 12 us  [hold_stacks_all(): return all_to_all(back, 'protos', pos_dim, pos_dim, tiled=True)]
    psum x3, blocking collectives: 120 us -> 108 us  [on_device(): col_scale = 1.0 / lax.psum(col_part, 'rows')]
  transfers between devices with their start and end apart: 2 -> 3, of which waited for: 2 -> 2; matrix products, arithmetic and copies ran while one was open for 1% -> 8% of each run, Pallas kernels for 0% -> 0%
where the time goes in v1:
time: 743 us; the launch traced here: 740 us
  blocking collectives  319 us (43%)
  waiting for transfers between devices  264 us (36%)
  matrix products  66.9 us (9%)
  other arithmetic  57.9 us (8%)
  between operations  14.1 us (2%)
  starting transfers between devices  12.1 us (2%)
    reduce_scatter x1, waiting for transfers between devices, on_device(): lax.psum_scatter(feature_term, 'protos', scatter_dimension=0, tiled=True)  213 us
    psum x3, blocking collectives, on_device(): row_whole = lax.psum(row_part, 'protos')  173 us
    psum x3, blocking collectives, on_device(): col_scale = 1.0 / lax.psum(col_part, 'rows')  108 us
    reduce_scatter x1, waiting for transfers between devices, on_device(): lax.psum_scatter(term.reshape(row_groups, block, term.shape[1]), 'rows',...  51.1 us
    unnamed x31, other arithmetic  42.7 us
    all_gather x1, blocking collectives, on_device(): lax.all_gather(local_t, 'protos', axis=0, tiled=True)  38.8 us
    dot_general x3, matrix products, on_device(): row_part = jnp.dot(kernel, col_scale, precision=lax.Precision.HIGHEST)  28.9 us
    dot_general x3, matrix products, on_device(): col_part = jnp.dot(row_scale, kernel, precision=lax.Precision.HIGHEST)  16.9 us
  transfers between devices with their start and end apart: 3, of which 2 were waited for; matrix products, arithmetic and copies ran while one was open for 8% of the time, Pallas kernels for 0%

profile of v1, /device:TPU:1, one launch (start us, length us, event | category | flops | bytes accessed | tf_op | source)
XLA Modules:
  0.0 739.6 jit_solution(3998740801087864482)
XLA Ops:
  8.0 1.4 constant_dynamic-update-slice_fusion.31
  13.5 1.4 constant_dynamic-update-slice_fusion.27
  14.9 1.4 constant_dynamic-update-slice_fusion.26
  16.3 1.4 constant_dynamic-update-slice_fusion.25
  17.7 1.4 constant_dynamic-update-slice_fusion.24
  19.0 1.4 constant_dynamic-update-slice_fusion.23
  20.4 1.4 constant_dynamic-update-slice_fusion.22
  21.8 1.4 constant_dynamic-update-slice_fusion.21
  23.2 1.4 constant_dynamic-update-slice_fusion.20
  24.5 1.4 constant_dynamic-update-slice_fusion.19
  25.9 1.4 constant_dynamic-update-slice_fusion.18
  27.3 1.4 constant_dynamic-update-slice_fusion.17
  28.7 1.4 constant_dynamic-update-slice_fusion.16
  30.1 1.4 constant_dynamic-update-slice_fusion.15
  31.4 1.4 constant_dynamic-update-slice_fusion.14
  39.7 1.4 constant_dynamic-update-slice_fusion.8
  41.1 1.4 constant_dynamic-update-slice_fusion.7
  42.5 1.4 constant_dynamic-update-slice_fusion.6
  43.8 1.4 constant_dynamic-update-slice_fusion.5
  45.2 1.4 constant_dynamic-update-slice_fusion.4
  46.6 1.4 constant_dynamic-update-slice_fusion.3
  48.0 1.4 constant_dynamic-update-slice_fusion.2
  49.4 1.4 constant_dynamic-update-slice_fusion.1
  50.7 1.4 constant_dynamic-update-slice_fusion
  52.1 12.0 %all-to-all-start = ((bf16[32,16,384]{2,1,0:T(8,128)(2,1)}), bf16[32,16,384]{2,1,0:T(8,128)(2,1)S(1)}, u32[]{:S(2)}, u32[]{:S(2)}) async-start(bf16[32,16,384]{2,1,0:T(8,128)(2,1)} %bitcast), calls=%async_computation | async-start | bytes 786432 | tf_op jit(solution)/shard_map/all_to_all | solution.py:18
  65.8 2.6 fusion.1
  68.4 38.8 %all_gather.3 = bf16[512,384]{1,0:T(8,128)(2,1)S(1)} all-gather(bf16[16,384]{1,0:T(8,128)(2,1)S(1)} %fusion.6), channel_id=1, replica_groups=mesh['rows'=8,'protos'=32] {'protos'}, dimensions={0}, use_global_device_ids=true | all-gather | bytes 405504 | tf_op jit(solution)/shard_map/all_gather | solution.py:42
  107.2 4.3 multiply_exponential_fusion
  111.5 3.2 copy-done
  114.8 4.0 fusion.7
  118.8 32.9 %psum.50 = f32[4096]{0:T(1024)S(1)} all-reduce(f32[4096]{0:T(1024)S(1)} %bitcast.38), channel_id=1, replica_groups=mesh['rows'=8,'protos'=32] {'rows'}, use_global_device_ids=true, to_apply=%region_5.0 | all-reduce | flops 4096 | bytes 32768 | tf_op jit(solution)/shard_map/psum | solution.py:51
  151.7 9.4 %fusion.14 = f32[1,512]{1,0:T(1,128)S(1)} fusion(f32[512,4096]{1,0:T(8,128)} %copy-done, f32[4096,1]{0,1:T(1,128)S(1)} %bitcast.34), kind=kOutput, calls=%fused_computation.63 | convolution fusion | flops 25165824 | bytes 8407040 | tf_op jit(solution)/shard_map/dot_general | solution.py:52
  161.2 58.6 %psum.51 = f32[512]{0:T(512)S(1)} all-reduce(f32[512]{0:T(512)S(1)} %bitcast.40), channel_id=1, replica_groups=mesh['rows'=8,'protos'=32] {'protos'}, use_global_device_ids=true, to_apply=%region_6.0 | all-reduce | flops 512 | bytes 4096 | tf_op jit(solution)/shard_map/psum | solution.py:54
  219.8 6.3 fusion.15
  226.1 37.4 %psum.52 = f32[4096]{0:T(1024)S(1)} all-reduce(f32[4096]{0:T(1024)S(1)} %bitcast.35), channel_id=1, replica_groups=mesh['rows'=8,'protos'=32] {'rows'}, use_global_device_ids=true, to_apply=%region_7.0 | all-reduce | flops 4096 | bytes 32768 | tf_op jit(solution)/shard_map/psum | solution.py:51
  263.6 9.4 %fusion.16 = f32[1,512]{1,0:T(1,128)S(1)} fusion(f32[512,4096]{1,0:T(8,128)} %copy-done, f32[4096,1]{0,1:T(1,128)S(1)} %bitcast.36), kind=kOutput, calls=%fused_computation.65 | convolution fusion | flops 25165824 | bytes 8407040 | tf_op jit(solution)/shard_map/dot_general | solution.py:52
  273.0 55.8 %psum.53 = f32[512]{0:T(512)S(1)} all-reduce(f32[512]{0:T(512)S(1)} %bitcast.42), channel_id=1, replica_groups=mesh['rows'=8,'protos'=32] {'protos'}, use_global_device_ids=true, to_apply=%region_8.0 | all-reduce | flops 512 | bytes 4096 | tf_op jit(solution)/shard_map/psum | solution.py:56
  328.8 6.5 fusion.17
  335.3 37.6 %psum.54 = f32[4096]{0:T(1024)} all-reduce(f32[4096]{0:T(1024)S(1)} %bitcast.37), channel_id=1, replica_groups=mesh['rows'=8,'protos'=32] {'rows'}, use_global_device_ids=true, to_apply=%region_9.0 | all-reduce | flops 4096 | bytes 32768 | tf_op jit(solution)/shard_map/psum | solution.py:51
  373.6 10.0 %fusion.18 = f32[1,512]{1,0:T(1,128)} fusion(f32[512,4096]{1,0:T(8,128)} %copy-done, f32[4096,1]{0,1:T(1,128)S(1)} %bitcast.33), kind=kOutput, calls=%fused_computation.67 | convolution fusion | flops 25165824 | bytes 8407040 | tf_op jit(solution)/shard_map/dot_general | solution.py:52
  383.7 6.2 fusion
  389.9 58.2 %all-reduce = (f32[512]{0:T(512)}, f32[512]{0:T(512)}) all-reduce(f32[512]{0:T(512)} %bitcast.39, f32[512]{0:T(512)} %get-tuple-element.4), channel_id=1, replica_groups=mesh['rows'=8,'protos'=32] {'protos'}, use_global_device_ids=true, to_apply=%region_10.0 | all-reduce | flops 1024 | bytes 8192 | tf_op jit(solution)/shard_map/psum | solution.py:56
  448.7 7.3 subtract_convert_fusion
  456.1 2.0 copy-done.2
  458.1 3.3 convolution_multiply_fusion.1
  461.5 7.2 convolution_multiply_fusion
  468.8 212.9 %reduce-scatter.3.cloned.1.call-done = f32[16,384]{1,0:T(8,128)} async-done(((f32[512,384]{1,0:T(8,128)}), f32[16,384]{1,0:T(8,128)}) %reduce-scatter.3.cloned.1.call-update) | async-done | bytes 24592 | tf_op jit(solution)/shard_map/reduce_scatter | solution.py:62
  681.6 51.1 %reduce-scatter.5.cloned.1.call-done = f32[1,512,384]{2,1,0:T(8,128)} async-done(((f32[8,512,384]{2,1,0:T(8,128)}), f32[1,512,384]{2,1,0:T(8,128)}) %reduce-scatter.5.cloned.1.call-update) | async-done | bytes 786448 | tf_op jit(solution)/shard_map/reduce_scatter | solution.py:70
  (33 shorter events, 15.0 us)
Async XLA Ops:
  52.1 331.5 %all-to-all-start = ((bf16[32,16,384]{2,1,0:T(8,128)(2,1)}), bf16[32,16,384]{2,1,0:T(8,128)(2,1)S(1)}, u32[]{:S(2)}, u32[]{:S(2)}) async-start(bf16[32,16,384]{2,1,0:T(8,128)(2,1)} %bitcast), calls=%async_computation | async-start | bytes 786432 | tf_op jit(solution)/shard_map/all_to_all | solution.py:18
  64.1 617.5 %reduce-scatter.3.cloned.1.call-start = ((), (), s32[]{:S(2)}) async-start(), calls=%async_computation.3 | async-start | bytes 811008 | tf_op jit(solution)/shard_map/reduce_scatter | solution.py:62
  68.4 50.4 %copy-start.3 = (f32[4096]{0:T(1024)}, f32[4096]{0:T(1024)S(1)}, u32[]{:S(2)}) copy-start(f32[4096]{0:T(1024)S(1)} %add_rsqrt_fusion) | copy-start | bytes 49156
  111.5 3.2 copy-start
  328.8 54.9 %copy-start.1 = (bf16[4096,384]{1,0:T(8,128)(2,1)S(1)}, bf16[4096,384]{1,0:T(8,128)(2,1)}, u32[]{:S(2)}) copy-start(bf16[4096,384]{1,0:T(8,128)(2,1)} %param.5) | copy-start | bytes 9437188
  448.7 9.4 %copy-start.4 = (f32[4096]{0:T(1024)S(1)}, f32[4096]{0:T(1024)}, u32[]{:S(2)}) copy-start(f32[4096]{0:T(1024)} %copy-done.3) | copy-start | bytes 49156
  456.1 2.0 copy-start.2
  461.5 271.3 %reduce-scatter.5.cloned.1.call-start = ((), (), s32[]{:S(2)}) async-start(), calls=%async_computation.4 | async-start | bytes 7077888 | tf_op jit(solution)/shard_map/reduce_scatter | solution.py:70
Sparse Core Ops, SparseCore 0:
  461.6 220.0 reduce-scatter.2
  684.8 47.9 reduce-scatter.4
